TPU v7x, 256 devices: a whole 4x4x8 slice. The times are simulated.
256 devices in a mesh: row: 8 (over y_lo, x), col: 32 (over z, y_hi, core).
Axes of the slice: x: 4, y: 4 (y_hi: 2, y_lo: 2; y = y_hi * 2 + y_lo), z: 8, core: 2. Of those that a mesh axis runs over, the one named last changes fastest.
Arguments:
- pair_rep: float32 [256, 256, 128], P('row', 'col'), may hold values from -160 to 160
- ln_gain: float32 [128], replicated, may hold values from 0.25 to 1.75
- ln_bias: float32 [128], replicated, may hold values from -3 to 3
- w_in: float32 [1024, 128], replicated, may hold values from -0.5 to 0.5
- w_out: float32 [512, 128], replicated, may hold values from -0.25 to 0.25
- w_pde: float32 [128, 64], replicated, may hold values from -2 to 2
- labels: int32 [256, 256], P('row', 'col'), may hold values from 0 to 63
- pair_mask: int32 [256, 256], P('row', 'col'), may hold values from 0 to 1, as said below
Outputs:
- mean_loss: float32 [], replicated
- d_pair_rep: float32 [256, 256, 128], P('row', 'col')
- d_ln_gain: float32 [128], replicated
- d_ln_bias: float32 [128], replicated
- d_w_in: float32 [1024, 128], P(('row', 'col'))
- d_w_out: float32 [512, 128], P(('row', 'col'))
- d_w_pde: float32 [128, 64], replicated
Inputs may be any that keep to these rules, and one draw needn't show every extreme that they name: pair_mask[i][j] = m_i m_j for a flag m_i of token i, with m_i = 1 whenever i is a multiple of 16.
All inputs are finite; a program needn't handle non-finite values.
Results may differ from a plain program's by a relative error of at most 0.0003.
Values sent between devices are 32-bit elements; how exact they have to be, the bound alone decides.
No kernel may reach another device: no remote copies, remote signals or barrier semaphores. Data moves between devices by JAX's collectives and lax.ppermute only.
A program may use at most 64 MiB of HBM per device.

v0:
```python
import jax
import jax.numpy as jnp
from jax import lax
from jax.sharding import Mesh
from jax.sharding import PartitionSpec as P

ROW = ("row_0", "row_1")
COL = ("col_0", "col_1", "col_2")
ROW_COL = ("row_0", "row_1", "col_0", "col_1", "col_2")
epsilon = 1e-05


def over_axes(shard, axes):
    for axis in axes:
        shard = lax.psum(shard, axis)
    return shard


def in_blocks(shard, dim, size):
    before, after = (shard.shape[:dim], shard.shape[dim + 1 :])
    return jnp.moveaxis(shard.reshape(*before, size, -1, *after), dim, 0)


def sent_and_summed(shard, axis, dim):
    tiles = in_blocks(shard, dim, lax.axis_size(axis))
    arrived = lax.all_to_all(tiles, axis, split_axis=0, concat_axis=0, tiled=True)
    return arrived.sum(axis=0)


def transition(rows_block, ln_gain, ln_bias, w_in, w_out):
    average = jnp.mean(rows_block, axis=-1, keepdims=True)
    centred = rows_block - average
    variance = jnp.mean(centred * centred, axis=-1, keepdims=True)
    normed = centred * lax.rsqrt(variance + epsilon) * ln_gain + ln_bias
    projected_in = lax.dot_general(
        normed,
        w_in,
        (((1,), (1,)), ((), ())),
        precision=lax.Precision.HIGHEST,
        preferred_element_type=jnp.float32,
    )
    hidden_units = w_out.shape[0]
    hidden = jax.nn.silu(projected_in[:, :hidden_units]) * projected_in[:, hidden_units:]
    return rows_block + jnp.dot(
        hidden, w_out, precision=lax.Precision.HIGHEST, preferred_element_type=jnp.float32
    )


def group_rows(tile_rows, tile_cols):
    stride_rows = 1
    while (
        stride_rows < tile_rows
        and stride_rows * tile_cols < 1024
        and (tile_rows % (stride_rows * 2) == 0)
    ):
        stride_rows = stride_rows * 2
    return stride_rows


def mirror(tile):
    row_devices = lax.axis_size(ROW)
    col_devices = lax.axis_size(COL)
    factor = col_devices // row_devices
    tile_cols = tile.shape[1]
    channels = tile.shape[2]
    slab_rows = tile_cols // row_devices
    pieces = tile.reshape(factor, row_devices, slab_rows, tile_cols * channels)
    pieces = lax.all_to_all(
        lax.all_to_all(pieces, ROW, split_axis=1, concat_axis=0, tiled=True),
        COL,
        split_axis=0,
        concat_axis=0,
        tiled=True,
    )
    pieces = pieces.reshape(row_devices, factor, slab_rows, tile_cols * channels)
    pieces = lax.all_to_all(pieces, ROW, split_axis=0, concat_axis=2, tiled=True)
    pieces = pieces.reshape(factor, tile_cols, tile_cols, channels)
    return jnp.transpose(pieces, (0, 2, 1, 3)).reshape(factor * tile_cols, tile_cols, channels)


def on_device(pair_rep, ln_gain, ln_bias, w_in, w_out, w_pde, labels, pair_mask):
    tile_rows, tile_cols, channels = pair_rep.shape
    stride_rows = group_rows(tile_rows, tile_cols)
    blocks = pair_rep.reshape(tile_rows // stride_rows, stride_rows * tile_cols, channels)

    def forward(rows_block):
        return transition(rows_block, ln_gain, ln_bias, w_in, w_out)

    updated = lax.map(forward, blocks).reshape(tile_rows, tile_cols, channels)
    mask_float = pair_mask.astype(jnp.float32)
    local_count = jnp.sum(mask_float)
    valid_count = over_axes(local_count, ROW_COL)
    inverse_count = 1.0 / valid_count
    projected = jnp.einsum("ijc,cb->ijb", updated, w_pde, precision=lax.Precision.HIGHEST)
    scores = projected + mirror(projected)
    highest = jnp.max(scores, axis=-1, keepdims=True)
    shifted = jnp.exp(scores - highest)
    exp_total = jnp.sum(shifted, axis=-1, keepdims=True)
    log_total = highest + jnp.log(exp_total)
    bin_index = lax.broadcasted_iota(jnp.int32, (1, 1, scores.shape[2]), 2)
    onehot = (labels[:, :, None] == bin_index).astype(jnp.float32)
    picked = jnp.sum(scores * onehot, axis=-1, keepdims=True)
    local_loss = jnp.sum(mask_float * (log_total - picked)[:, :, 0])
    d_scores = mask_float[:, :, None] * (shifted / exp_total - onehot) * inverse_count
    d_sym = d_scores + mirror(d_scores)
    d_updated = jnp.einsum("ijb,cb->ijc", d_sym, w_pde, precision=lax.Precision.HIGHEST)
    grad_pde = jnp.einsum("ijc,ijb->cb", updated, d_sym, precision=lax.Precision.HIGHEST)
    cot_blocks = d_updated.reshape(blocks.shape)

    def backward(totals, pieces):
        rows_block, cotangent = pieces
        outcome, pullback = jax.vjp(transition, rows_block, ln_gain, ln_bias, w_in, w_out)
        gradients = pullback(cotangent)
        merged = tuple((earlier + later for earlier, later in zip(totals, gradients[1:])))
        return (merged, gradients[0])

    start_sums = (
        jnp.zeros_like(ln_gain),
        jnp.zeros_like(ln_bias),
        jnp.zeros_like(w_in),
        jnp.zeros_like(w_out),
    )
    param_sums, d_blocks = lax.scan(backward, start_sums, (blocks, cot_blocks))
    g_gain, g_bias, g_in, g_out = param_sums
    row_in, row_out = (sent_and_summed(g_in, ROW, 0), sent_and_summed(g_out, ROW, 0))
    shard_in, shard_out = (sent_and_summed(row_in, COL, 0), sent_and_summed(row_out, COL, 0))
    loss_sum, gain_sum, bias_sum, pde_sum = (
        over_axes(local_loss, ROW_COL),
        over_axes(g_gain, ROW_COL),
        over_axes(g_bias, ROW_COL),
        over_axes(grad_pde, ROW_COL),
    )
    late_scale = 1.0
    mean_loss = loss_sum / valid_count
    d_pair_rep = d_blocks.reshape(pair_rep.shape) * late_scale
    return (
        mean_loss,
        d_pair_rep,
        gain_sum * late_scale,
        bias_sum * late_scale,
        shard_in * late_scale,
        shard_out * late_scale,
        pde_sum * late_scale,
    )


def solution(mesh):
    torus = Mesh(mesh.devices.reshape(2, 4, 8, 2, 2), ("row_0", "row_1", "col_0", "col_1", "col_2"))
    return jax.shard_map(
        on_device,
        mesh=torus,
        in_specs=(P(ROW, COL, None), P(), P(), P(), P(), P(), P(ROW, COL), P(ROW, COL)),
        out_specs=(P(), P(ROW, COL, None), P(), P(), P(ROW_COL, None), P(ROW_COL, None), P()),
        check_vma=False,
    )
```

profile of v0, /device:TPU:1, one launch (start us, length us, event | category | flops | bytes accessed | tf_op | source)
XLA Modules:
  0.0 250.9 jit_solution(8225384277171636121)
XLA Ops:
  6.1 10.9 %all_to_all.96 = f32[4,8,1,512]{3,0,2,1:T(4,128)S(1)} all-to-all(f32[4,8,1,512]{3,0,2,1:T(4,128)S(1)} %copy.66), channel_id=1, replica_groups=mesh['row_0'=2,'row_1'=4,'col_0'=8,'col_1'=2,'col_2'=2] {'row_0','row_1'}, dimensions={1} | all-to-all | bytes 131072 | tf_op jit(solution)/shard_map/all_to_all | solution.py:69
  17.0 22.7 %all_to_all.97 = f32[32,1,1,512]{3,2,1,0:T(1,128)S(1)} all-to-all(f32[32,1,1,512]{3,2,1,0:T(1,128)S(1)} %bitcast.101), channel_id=1, replica_groups=mesh['row_0'=2,'row_1'=4,'col_0'=8,'col_1'=2,'col_2'=2] {'col_0','col_1'..., dimensions={0} | all-to-all | bytes 131072 | tf_op jit(solution)/shard_map/all_to_all | solution.py:68
  40.3 3.5 %all-to-all-start.2 = ((f32[8,4,1,512]{3,1,2,0:T(4,128)}), f32[8,4,1,512]{3,1,2,0:T(4,128)S(1)}, u32[]{:S(2)}, u32[]{:S(2)}) async-start(f32[8,4,1,512]{3,1,2,0:T(4,128)} %copy.68), calls=%async_computation.2 | async-start | bytes 131072 | tf_op jit(solution)/shard_map/all_to_all | solution.py:76
  44.6 4.4 %all-to-all-done.2 = f32[8,4,1,512]{3,1,2,0:T(4,128)S(1)} async-done(((f32[8,4,1,512]{3,1,2,0:T(4,128)}), f32[8,4,1,512]{3,1,2,0:T(4,128)S(1)}, u32[]{:S(2)}, u32[]{:S(2)}) %all-to-all-start.2) | async-done | bytes 65568 | tf_op jit(solution)/shard_map/all_to_all | solution.py:76
  50.1 4.4 %psum.180 = f32[]{:T(128)} all-reduce(f32[]{:T(128)} %get-tuple-element.57), channel_id=1, replica_groups=mesh['row_0'=2,'row_1'=4,'col_0'=8,'col_1'=2,'col_2'=2] {'row_0'}, use_global_device_ids=true, to_apply=%region_12.13 | all-reduce | flops 1 | bytes 8 | tf_op jit(solution)/shard_map/psum | solution.py:15
  54.5 7.6 %psum.181 = f32[]{:T(128)} all-reduce(f32[]{:T(128)} %psum.180), channel_id=1, replica_groups=mesh['row_0'=2,'row_1'=4,'col_0'=8,'col_1'=2,'col_2'=2] {'row_1'}, use_global_device_ids=true, to_apply=%region_13.14 | all-reduce | flops 1 | bytes 8 | tf_op jit(solution)/shard_map/psum | solution.py:15
  62.1 11.7 %psum.182 = f32[]{:T(128)} all-reduce(f32[]{:T(128)} %psum.181), channel_id=1, replica_groups=mesh['row_0'=2,'row_1'=4,'col_0'=8,'col_1'=2,'col_2'=2] {'col_0'}, use_global_device_ids=true, to_apply=%region_14.15 | all-reduce | flops 1 | bytes 8 | tf_op jit(solution)/shard_map/psum | solution.py:15
  73.7 5.9 %psum.183 = f32[]{:T(128)} all-reduce(f32[]{:T(128)} %psum.182), channel_id=1, replica_groups=mesh['row_0'=2,'row_1'=4,'col_0'=8,'col_1'=2,'col_2'=2] {'col_1'}, use_global_device_ids=true, to_apply=%region_15.16 | all-reduce | flops 1 | bytes 8 | tf_op jit(solution)/shard_map/psum | solution.py:15
  79.6 12.7 %psum.184 = f32[]{:T(128)} all-reduce(f32[]{:T(128)} %psum.183), channel_id=1, replica_groups=mesh['row_0'=2,'row_1'=4,'col_0'=8,'col_1'=2,'col_2'=2] {'col_2'}, use_global_device_ids=true, to_apply=%region_16.17 | all-reduce | flops 1 | bytes 8 | tf_op jit(solution)/shard_map/psum | solution.py:15
  93.4 7.6 %all_to_all.98 = f32[4,8,1,512]{3,0,2,1:T(4,128)S(1)} all-to-all(f32[4,8,1,512]{3,0,2,1:T(4,128)S(1)} %copy.72), channel_id=1, replica_groups=mesh['row_0'=2,'row_1'=4,'col_0'=8,'col_1'=2,'col_2'=2] {'row_0','row_1'}, dimensions={1} | all-to-all | bytes 131072 | tf_op jit(solution)/shard_map/all_to_all | solution.py:69
  101.0 15.4 %all_to_all.99 = f32[32,1,1,512]{3,2,1,0:T(1,128)S(1)} all-to-all(f32[32,1,1,512]{3,2,1,0:T(1,128)S(1)} %bitcast.104), channel_id=1, replica_groups=mesh['row_0'=2,'row_1'=4,'col_0'=8,'col_1'=2,'col_2'=2] {'col_0','col_1'..., dimensions={0} | all-to-all | bytes 131072 | tf_op jit(solution)/shard_map/all_to_all | solution.py:68
  116.5 7.6 %all_to_all.100 = f32[8,4,1,512]{3,1,2,0:T(4,128)S(1)} all-to-all(f32[8,4,1,512]{3,1,2,0:T(4,128)S(1)} %copy.74), channel_id=1, replica_groups=mesh['row_0'=2,'row_1'=4,'col_0'=8,'col_1'=2,'col_2'=2] {'row_0','row_1'}, dimensions={0} | all-to-all | bytes 131072 | tf_op jit(solution)/shard_map/all_to_all | solution.py:76
  129.6 4.0 %all-to-all-start.8 = ((f32[8,64,128]{2,1,0:T(8,128)}), f32[8,64,128]{2,1,0:T(8,128)}, u32[]{:S(2)}, u32[]{:S(2)}) async-start(f32[8,64,128]{2,1,0:T(8,128)} %fusion.7), calls=%async_computation.8 | async-start | bytes 524288 | tf_op jit(solution)/shard_map/all_to_all | solution.py:26
  134.8 2.7 %fusion.9 = f32[8,128,128]{2,1,0:T(8,128)} fusion(f32[8,128,256]{2,1,0:T(8,128)S(1)} %bitcast.94, f32[32,8,128]{2,1,0:T(8,128)S(1)} %copy-done.1, f32[128]{0:T(128)S(1)} %copy-done.18, f32[128]{0:T(128)S(1)} %copy-done.14, f32[32,8]{1,0:T(8,128)} %get-tuple-element.98, f32[32,8]{1,0:T(8,128)S(1)} %broadcast_multiply_fusion), kind=kOutput, calls=%fused_computation.16 | convolution fusion | flops 402784256 | bytes 1707008 | tf_op jit(solution)/shard_map/while/body/eval_jaxpr/transpose(jvp())/dot_general | solution.py:35
  140.1 3.5 %all-to-all-start.6 = ((f32[8,128,128]{2,1,0:T(8,128)}), f32[8,128,128]{2,1,0:T(8,128)S(1)}, u32[]{:S(2)}, u32[]{:S(2)}) async-start(f32[8,128,128]{2,1,0:T(8,128)} %fusion.9), calls=%async_computation.6 | async-start | bytes 1048576 | tf_op jit(solution)/shard_map/all_to_all | solution.py:26
  146.2 5.5 %all-to-all-done.6 = f32[8,128,128]{2,1,0:T(8,128)S(1)} async-done(((f32[8,128,128]{2,1,0:T(8,128)}), f32[8,128,128]{2,1,0:T(8,128)S(1)}, u32[]{:S(2)}, u32[]{:S(2)}) %all-to-all-start.6) | async-done | bytes 524320 | tf_op jit(solution)/shard_map/all_to_all | solution.py:26
  151.7 6.5 %all-to-all-start.9 = ((f32[32,2,128]{2,1,0:T(2,128)}), f32[32,2,128]{2,1,0:T(2,128)S(1)}, u32[]{:S(2)}, u32[]{:S(2)}) async-start(f32[32,2,128]{2,1,0:T(2,128)} %bitcast.29), calls=%async_computation.9 | async-start | bytes 65536 | tf_op jit(solution)/shard_map/all_to_all | solution.py:26
  158.6 7.2 %all-reduce.6 = (f32[]{:T(128)}, f32[128]{0:T(128)S(1)}, f32[128]{0:T(128)S(1)}, f32[128,64]{0,1:T(8,128)S(1)}) all-reduce(f32[]{:T(128)} %get-tuple-element.58, f32[128]{0:T(128)S(1)} %get-tuple-element.52, f32[128]{0:T(128)S(1)} %get-tuple-element.54, ...), channel_id=1, replica_groups=mesh['row_0'=2,'row_1'=4,'col_0'=8,'col_1'=2,'col_2'=2] {'row_0'}, use_global_device_ids=true, to_apply=%region_6.7 | all-reduce | flops 8449 | bytes 67592 | tf_op jit(solution)/shard_map/psum | solution.py:15
  165.8 13.7 %all-reduce.3 = (f32[]{:T(128)}, f32[128]{0:T(128)S(1)}, f32[128]{0:T(128)S(1)}, f32[128,64]{0,1:T(8,128)S(1)}) all-reduce(f32[]{:T(128)} %get-tuple-element.87, f32[128]{0:T(128)S(1)} %get-tuple-element.88, f32[128]{0:T(128)S(1)} %get-tuple-element.89, ...), channel_id=1, replica_groups=mesh['row_0'=2,'row_1'=4,'col_0'=8,'col_1'=2,'col_2'=2] {'row_1'}, use_global_device_ids=true, to_apply=%region_7.8 | all-reduce | flops 8449 | bytes 67592 | tf_op jit(solution)/shard_map/psum | solution.py:15
  179.4 23.6 %all-reduce.2 = (f32[]{:T(128)}, f32[128]{0:T(128)S(1)}, f32[128]{0:T(128)S(1)}, f32[128,64]{0,1:T(8,128)S(1)}) all-reduce(f32[]{:T(128)} %get-tuple-element.63, f32[128]{0:T(128)S(1)} %get-tuple-element.76, f32[128]{0:T(128)S(1)} %get-tuple-element.77, ...), channel_id=1, replica_groups=mesh['row_0'=2,'row_1'=4,'col_0'=8,'col_1'=2,'col_2'=2] {'col_0'}, use_global_device_ids=true, to_apply=%region_8.9 | all-reduce | flops 8449 | bytes 67592 | tf_op jit(solution)/shard_map/psum | solution.py:15
  203.1 10.6 %all-reduce.5 = (f32[]{:T(128)}, f32[128]{0:T(128)S(1)}, f32[128]{0:T(128)S(1)}, f32[128,64]{0,1:T(8,128)S(1)}) all-reduce(f32[]{:T(128)} %get-tuple-element.59, f32[128]{0:T(128)S(1)} %get-tuple-element.60, f32[128]{0:T(128)S(1)} %get-tuple-element.61, ...), channel_id=1, replica_groups=mesh['row_0'=2,'row_1'=4,'col_0'=8,'col_1'=2,'col_2'=2] {'col_1'}, use_global_device_ids=true, to_apply=%region_9.10 | all-reduce | flops 8449 | bytes 67592 | tf_op jit(solution)/shard_map/psum | solution.py:15
  213.7 19.8 %all-reduce.4 = (f32[]{:T(128)}, f32[128]{0:T(128)}, f32[128]{0:T(128)}, f32[128,64]{0,1:T(8,128)}) all-reduce(f32[]{:T(128)} %get-tuple-element.83, f32[128]{0:T(128)S(1)} %get-tuple-element.84, f32[128]{0:T(128)S(1)} %get-tuple-element.85, ...), channel_id=1, replica_groups=mesh['row_0'=2,'row_1'=4,'col_0'=8,'col_1'=2,'col_2'=2] {'col_2'}, use_global_device_ids=true, to_apply=%region_10.11 | all-reduce | flops 8449 | bytes 67592 | tf_op jit(solution)/shard_map/psum | solution.py:15
  235.5 3.8 %all-to-all-start.7 = ((f32[32,4,128]{2,1,0:T(4,128)}), f32[32,4,128]{2,1,0:T(4,128)S(1)}, u32[]{:S(2)}, u32[]{:S(2)}) async-start(f32[32,4,128]{2,1,0:T(4,128)} %bitcast.25), calls=%async_computation.7 | async-start | bytes 131072 | tf_op jit(solution)/shard_map/all_to_all | solution.py:26
  240.7 8.5 %all-to-all-done.7 = f32[32,4,128]{2,1,0:T(4,128)S(1)} async-done(((f32[32,4,128]{2,1,0:T(4,128)}), f32[32,4,128]{2,1,0:T(4,128)S(1)}, u32[]{:S(2)}, u32[]{:S(2)}) %all-to-all-start.7) | async-done | bytes 65568 | tf_op jit(solution)/shard_map/all_to_all | solution.py:26
  (92 shorter events, 23.2 us)
Async XLA Ops:
  0.6 2.7 %copy-start = (f32[1024,128]{1,0:T(8,128)S(1)}, f32[1024,128]{1,0:T(8,128)}, u32[]{:S(2)}) copy-start(f32[1024,128]{1,0:T(8,128)} %param.11) | copy-start | bytes 1572868
  0.6 1.2 copy-start.1
  1.9 0.9 copy-start.7
  2.8 0.7 copy-start.13
  2.8 0.7 copy-start.17
  3.4 1.0 copy-start.9
  3.4 1.0 copy-start.19
  4.5 0.8 copy-start.6
  40.3 3.5 %copy-start.15 = (s32[32,8]{0,1:T(8,128)S(1)}, s32[32,8]{0,1:T(8,128)}, u32[]{:S(2)}) copy-start(s32[32,8]{0,1:T(8,128)} %param.14) | copy-start | bytes 3076
  40.3 8.6 %all-to-all-start.2 = ((f32[8,4,1,512]{3,1,2,0:T(4,128)}), f32[8,4,1,512]{3,1,2,0:T(4,128)S(1)}, u32[]{:S(2)}, u32[]{:S(2)}) async-start(f32[8,4,1,512]{3,1,2,0:T(4,128)} %copy.68), calls=%async_computation.2 | async-start | bytes 131072 | tf_op jit(solution)/shard_map/all_to_all | solution.py:76
  43.8 0.7 copy-start.16
  124.4 1.0 copy-start.20
  126.9 6.8 %copy-start.2 = (f32[256,512]{1,0:T(8,128)}, f32[256,512]{1,0:T(8,128)S(1)}, u32[]{:S(2)}) copy-start(f32[256,512]{1,0:T(8,128)S(1)} %get-tuple-element.96) | copy-start | bytes 1572868
  129.6 10.5 %all-to-all-start.8 = ((f32[8,64,128]{2,1,0:T(8,128)}), f32[8,64,128]{2,1,0:T(8,128)}, u32[]{:S(2)}, u32[]{:S(2)}) async-start(f32[8,64,128]{2,1,0:T(8,128)} %fusion.7), calls=%async_computation.8 | async-start | bytes 524288 | tf_op jit(solution)/shard_map/all_to_all | solution.py:26
  134.1 0.7 copy-start.14
  134.1 0.7 copy-start.18
  134.8 2.7 %copy-start.3 = (f32[256,512]{1,0:T(8,128)S(1)}, f32[256,512]{1,0:T(8,128)}, u32[]{:S(2)}) copy-start(f32[256,512]{1,0:T(8,128)} %copy-done.2) | copy-start | bytes 1572868
  134.8 2.7 %copy-start.8 = (f32[256]{0:T(256)S(1)}, f32[256]{0:T(256)}, u32[]{:S(2)}) copy-start(f32[256]{0:T(256)} %copy-done.7) | copy-start | bytes 3076
  134.8 2.7 %copy-start.10 = (f32[256]{0:T(256)S(1)}, f32[256]{0:T(256)}, u32[]{:S(2)}) copy-start(f32[256]{0:T(256)} %copy-done.9) | copy-start | bytes 3076
  140.1 11.5 %all-to-all-start.6 = ((f32[8,128,128]{2,1,0:T(8,128)}), f32[8,128,128]{2,1,0:T(8,128)S(1)}, u32[]{:S(2)}, u32[]{:S(2)}) async-start(f32[8,128,128]{2,1,0:T(8,128)} %fusion.9), calls=%async_computation.6 | async-start | bytes 1048576 | tf_op jit(solution)/shard_map/all_to_all | solution.py:26
  143.6 0.7 copy-start.12
  144.6 13.6 %copy-start.5 = (f32[32,8,128]{2,1,0:T(8,128)S(1)}, f32[32,8,128]{2,1,0:T(8,128)}, u32[]{:S(2)}) copy-start(f32[32,8,128]{2,1,0:T(8,128)} %copy-done.4) | copy-start | bytes 393220
  151.7 83.8 %all-to-all-start.9 = ((f32[32,2,128]{2,1,0:T(2,128)}), f32[32,2,128]{2,1,0:T(2,128)S(1)}, u32[]{:S(2)}, u32[]{:S(2)}) async-start(f32[32,2,128]{2,1,0:T(2,128)} %bitcast.29), calls=%async_computation.9 | async-start | bytes 65536 | tf_op jit(solution)/shard_map/all_to_all | solution.py:26
  235.5 13.6 %all-to-all-start.7 = ((f32[32,4,128]{2,1,0:T(4,128)}), f32[32,4,128]{2,1,0:T(4,128)S(1)}, u32[]{:S(2)}, u32[]{:S(2)}) async-start(f32[32,4,128]{2,1,0:T(4,128)} %bitcast.25), calls=%async_computation.7 | async-start | bytes 131072 | tf_op jit(solution)/shard_map/all_to_all | solution.py:26
  (2 other events, 1.2 us)
where the time goes:
time: 252 us; the launch traced here: 251 us
  blocking collectives  181 us (72%)
  starting transfers between devices  21.3 us (8%)
  waiting for transfers between devices  19.9 us (8%)
  matrix products  9.15 us (4%)
  other arithmetic  7.86 us (3%)
  local copies, waits for them, and re-layouts  7.24 us (3%)
  between operations  4.2 us (2%)
    psum x10, blocking collectives, over_axes(): shard = lax.psum(shard, axis)  117 us
    all_to_all x2, blocking collectives, mirror(): lax.all_to_all(lax.all_to_all(pieces, ROW, split_axis=1, concat_axis=0, t...  38.1 us
    all_to_all x2, blocking collectives, mirror(): lax.all_to_all(pieces, ROW, split_axis=1, concat_axis=0, tiled=True)  18.4 us
    all_to_all x4, starting transfers between devices, sent_and_summed(): lax.all_to_all(tiles, axis, split_axis=0, concat_axis=0, tiled=True)  17.8 us
    all_to_all x4, waiting for transfers between devices, sent_and_summed(): lax.all_to_all(tiles, axis, split_axis=0, concat_axis=0, tiled=True)  15.5 us
    all_to_all x1, blocking collectives, mirror(): lax.all_to_all(pieces, ROW, split_axis=0, concat_axis=2, tiled=True)  7.58 us
  transfers between devices with their start and end apart: 5, of which 4 were waited for; matrix products, arithmetic and copies ran while one was open for 3% of the time, Pallas kernels for 0%

commit v1 on v0

--- a/solution.py
+++ b/solution.py
@@ -12,7 +12,7 @@
 
 def over_axes(shard, axes):
     for axis in axes:
-        shard = lax.psum(shard, axis)
+        shard = jnp.sum(lax.all_gather(shard, axis), axis=0)
     return shard
 
 

time: 252 us -> 309 us (1.23)
  blocking collectives: 181 us -> 207 us
  starting transfers between devices: 21.3 us -> 37 us
  local copies, waits for them, and re-layouts: 7.24 us -> 22.1 us
  other arithmetic: 7.86 us -> 14.5 us
  waiting for transfers between devices: 19.9 us -> 14.7 us
    psum x10 -> x0, blocking collectives: 117 us -> none  [over_axes(): shard = lax.psum(shard, axis)]
    all_gather x0 -> x15, blocking collectives: none -> 112 us  [over_axes(): shard = jnp.sum(lax.all_gather(shard, axis), axis=0)]
    unnamed x0 -> x5, blocking collectives: none -> 39 us
    unnamed x44 -> x54, local copies, waits for them, and re-layouts: 3.93 us -> 19.3 us
    all_to_all x4, starting transfers between devices: 17.8 us -> 30.1 us  [sent_and_summed(): lax.all_to_all(tiles, axis, split_axis=0, concat_axis=0, tiled=True)]
    reduce_sum x0 -> x25, other arithmetic: none -> 8.23 us  [over_axes(): shard = jnp.sum(lax.all_gather(shard, axis), axis=0)]
    all_to_all x1 -> x0, blocking collectives: 7.58 us -> none  [mirror(): lax.all_to_all(pieces, ROW, split_axis=0, concat_axis=2, tiled=True)]
    all_to_all x4, waiting for transfers between devices: 15.5 us -> 8.48 us  [sent_and_summed(): lax.all_to_all(tiles, axis, split_axis=0, concat_axis=0, tiled=True)]
  transfers between devices with their start and end apart: 5 -> 6, of which waited for: 4 -> 3; matrix products, arithmetic and copies ran while one was open for 3% -> 3% of each run, Pallas kernels for 0% -> 0%
where the time goes in v1:
time: 309 us; the launch traced here: 307 us
  blocking collectives  207 us (67%)
  starting transfers between devices  37 us (12%)
  local copies, waits for them, and re-layouts  22.1 us (7%)
  waiting for transfers between devices  14.7 us (5%)
  other arithmetic  14.5 us (5%)
  matrix products  7.57 us (2%)
  between operations  4.23 us (1%)
    all_gather x15, blocking collectives, over_axes(): shard = jnp.sum(lax.all_gather(shard, axis), axis=0)  112 us
    unnamed x5, blocking collectives  39 us
    all_to_all x2, blocking collectives, mirror(): lax.all_to_all(lax.all_to_all(pieces, ROW, split_axis=1, concat_axis=0, t...  38.1 us
    all_to_all x4, starting transfers between devices, sent_and_summed(): lax.all_to_all(tiles, axis, split_axis=0, concat_axis=0, tiled=True)  30.1 us
    unnamed x54, local copies, waits for them, and re-layouts  19.3 us
    all_to_all x2, blocking collectives, mirror(): lax.all_to_all(pieces, ROW, split_axis=1, concat_axis=0, tiled=True)  18.4 us
    all_to_all x4, waiting for transfers between devices, sent_and_summed(): lax.all_to_all(tiles, axis, split_axis=0, concat_axis=0, tiled=True)  8.48 us
    reduce_sum x25, other arithmetic, over_axes(): shard = jnp.sum(lax.all_gather(shard, axis), axis=0)  8.23 us
  transfers between devices with their start and end apart: 6, of which 3 were waited for; matrix products, arithmetic and copies ran while one was open for 3% of the time, Pallas kernels for 0%

profile of v1, /device:TPU:1, one launch (start us, length us, event | category | flops | bytes accessed | tf_op | source)
XLA Modules:
  0.0 307.4 jit_solution(4822142222020462036)
XLA Ops:
  5.0 10.9 %all_to_all.96 = f32[4,8,1,512]{3,0,2,1:T(4,128)S(1)} all-to-all(f32[4,8,1,512]{3,0,2,1:T(4,128)S(1)} %copy.108), channel_id=1, replica_groups=mesh['row_0'=2,'row_1'=4,'col_0'=8,'col_1'=2,'col_2'=2] {'row_0','row_1'}, dimensions={1} | all-to-all | bytes 131072 | tf_op jit(solution)/shard_map/all_to_all | solution.py:69
  16.0 22.7 %all_to_all.97 = f32[32,1,1,512]{3,2,1,0:T(1,128)S(1)} all-to-all(f32[32,1,1,512]{3,2,1,0:T(1,128)S(1)} %bitcast.141), channel_id=1, replica_groups=mesh['row_0'=2,'row_1'=4,'col_0'=8,'col_1'=2,'col_2'=2] {'col_0','col_1'..., dimensions={0} | all-to-all | bytes 131072 | tf_op jit(solution)/shard_map/all_to_all | solution.py:68
  52.5 3.8 %all-reduce.16 = (f32[2]{0:T(128)S(1)}, f32[2]{0:T(128)S(1)}) all-reduce(f32[2]{0:T(128)S(1)} %dynamic-update-slice, f32[2]{0:T(128)S(1)} %dynamic-update-slice.5), channel_id=1, replica_groups=mesh['row_0'=2,'row_1'=4,'col_0'=8,'col_1'=2,'col_2'=2] {'row_0'}, use_global_device_ids=true, to_apply=%add.2 | all-reduce | flops 4 | bytes 32
  60.9 6.9 %all-reduce.13 = (f32[4]{0:T(128)S(1)}, f32[4]{0:T(128)S(1)}) all-reduce(f32[4]{0:T(128)S(1)} %dynamic-update-slice.1, f32[4]{0:T(128)S(1)} %dynamic-update-slice.6), channel_id=1, replica_groups=mesh['row_0'=2,'row_1'=4,'col_0'=8,'col_1'=2,'col_2'=2] {'row_1'}, use_global_device_ids=true, to_apply=%add.3 | all-reduce | flops 8 | bytes 64
  72.4 11.0 %all-reduce.12 = (f32[8]{0:T(128)S(1)}, f32[8]{0:T(128)S(1)}) all-reduce(f32[8]{0:T(128)S(1)} %dynamic-update-slice.2, f32[8]{0:T(128)S(1)} %dynamic-update-slice.7), channel_id=1, replica_groups=mesh['row_0'=2,'row_1'=4,'col_0'=8,'col_1'=2,'col_2'=2] {'col_0'}, use_global_device_ids=true, to_apply=%add.4 | all-reduce | flops 16 | bytes 128
  88.1 5.3 %all-reduce.15 = (f32[2]{0:T(128)S(1)}, f32[2]{0:T(128)S(1)}) all-reduce(f32[2]{0:T(128)S(1)} %dynamic-update-slice.3, f32[2]{0:T(128)S(1)} %dynamic-update-slice.8), channel_id=1, replica_groups=mesh['row_0'=2,'row_1'=4,'col_0'=8,'col_1'=2,'col_2'=2] {'col_1'}, use_global_device_ids=true, to_apply=%add.5 | all-reduce | flops 4 | bytes 32
  97.4 12.0 %all-reduce.14 = (f32[2]{0:T(128)S(1)}, f32[2]{0:T(128)S(1)}) all-reduce(f32[2]{0:T(128)S(1)} %dynamic-update-slice.4, f32[2]{0:T(128)S(1)} %dynamic-update-slice.9), channel_id=1, replica_groups=mesh['row_0'=2,'row_1'=4,'col_0'=8,'col_1'=2,'col_2'=2] {'col_2'}, use_global_device_ids=true, to_apply=%add.6 | all-reduce | flops 4 | bytes 32
  111.1 7.6 %all_to_all.98 = f32[4,8,1,512]{3,0,2,1:T(4,128)S(1)} all-to-all(f32[4,8,1,512]{3,0,2,1:T(4,128)S(1)} %copy.114), channel_id=1, replica_groups=mesh['row_0'=2,'row_1'=4,'col_0'=8,'col_1'=2,'col_2'=2] {'row_0','row_1'}, dimensions={1} | all-to-all | bytes 131072 | tf_op jit(solution)/shard_map/all_to_all | solution.py:69
  118.7 15.4 %all_to_all.99 = f32[32,1,1,512]{3,2,1,0:T(1,128)S(1)} all-to-all(f32[32,1,1,512]{3,2,1,0:T(1,128)S(1)} %bitcast.144), channel_id=1, replica_groups=mesh['row_0'=2,'row_1'=4,'col_0'=8,'col_1'=2,'col_2'=2] {'col_0','col_1'..., dimensions={0} | all-to-all | bytes 131072 | tf_op jit(solution)/shard_map/all_to_all | solution.py:68
  157.1 10.6 %all-gather.11 = f32[512,64]{0,1:T(8,128)S(1)} all-gather(f32[128,64]{0,1:T(8,128)S(1)} %reduce_sum.421), channel_id=13, replica_groups=mesh['row_0'=2,'row_1'=4,'col_0'=8,'col_1'=2,'col_2'=2] {'row_1'}, dimensions={0}, use_global_device_ids=true | all-gather | bytes 163840 | tf_op jit(solution)/shard_map/all_gather | solution.py:15
  167.8 3.9 %all-to-all-start.6 = ((f32[8,128,128]{2,1,0:T(8,128)}), f32[8,128,128]{2,1,0:T(8,128)S(1)}, u32[]{:S(2)}, u32[]{:S(2)}) async-start(f32[8,128,128]{2,1,0:T(8,128)} %fusion.9), calls=%async_computation.6 | async-start | bytes 1048576 | tf_op jit(solution)/shard_map/all_to_all | solution.py:26
  171.7 18.8 %all-gather.12 = f32[1024,64]{0,1:T(8,128)S(1)} all-gather(f32[128,64]{0,1:T(8,128)S(1)} %reduce_sum.422), channel_id=14, replica_groups=mesh['row_0'=2,'row_1'=4,'col_0'=8,'col_1'=2,'col_2'=2] {'col_0'}, dimensions={0}, use_global_device_ids=true | all-gather | bytes 294912 | tf_op jit(solution)/shard_map/all_gather | solution.py:15
  191.5 14.9 %all-to-all-start.9 = ((f32[32,2,128]{2,1,0:T(2,128)}), f32[32,2,128]{2,1,0:T(2,128)S(1)}, u32[]{:S(2)}, u32[]{:S(2)}) async-start(f32[32,2,128]{2,1,0:T(2,128)} %bitcast.54), calls=%async_computation.9 | async-start | bytes 65536 | tf_op jit(solution)/shard_map/all_to_all | solution.py:26
  206.4 5.3 %all-gather.13 = f32[256,64]{0,1:T(8,128)S(1)} all-gather(f32[128,64]{0,1:T(8,128)S(1)} %bitcast_reduce_fusion), channel_id=15, replica_groups=mesh['row_0'=2,'row_1'=4,'col_0'=8,'col_1'=2,'col_2'=2] {'col_1'}, dimensions={0}, use_global_device_ids=true | all-gather | bytes 98304 | tf_op jit(solution)/shard_map/all_gather | solution.py:15
  221.6 7.9 %all-gather.21 = f32[4,1,128]{2,1,0:T(1,128)S(1)} all-gather(f32[1,1,128]{2,1,0:T(1,128)S(1)} %bitcast.148), channel_id=8, replica_groups=mesh['row_0'=2,'row_1'=4,'col_0'=8,'col_1'=2,'col_2'=2] {'row_1'}, dimensions={0}, use_global_device_ids=true | all-gather | bytes 2560 | tf_op jit(solution)/shard_map/all_gather | solution.py:15
  229.5 5.2 %all-gather.16 = f32[4,1,128]{2,1,0:T(1,128)S(1)} all-gather(f32[1,1,128]{2,1,0:T(1,128)S(1)} %bitcast.147), channel_id=3, replica_groups=mesh['row_0'=2,'row_1'=4,'col_0'=8,'col_1'=2,'col_2'=2] {'row_1'}, dimensions={0}, use_global_device_ids=true | all-gather | bytes 2560 | tf_op jit(solution)/shard_map/all_gather | solution.py:15
  234.7 12.5 %all-gather.17 = f32[8,1,128]{2,1,0:T(1,128)S(1)} all-gather(f32[1,1,128]{2,1,0:T(1,128)S(1)} %bitcast.149), channel_id=4, replica_groups=mesh['row_0'=2,'row_1'=4,'col_0'=8,'col_1'=2,'col_2'=2] {'col_0'}, dimensions={0}, use_global_device_ids=true | all-gather | bytes 4608 | tf_op jit(solution)/shard_map/all_gather | solution.py:15
  247.2 4.6 %all-gather.18 = f32[2,1,128]{2,1,0:T(1,128)S(1)} all-gather(f32[1,1,128]{2,1,0:T(1,128)S(1)} %bitcast.150), channel_id=5, replica_groups=mesh['row_0'=2,'row_1'=4,'col_0'=8,'col_1'=2,'col_2'=2] {'col_1'}, dimensions={0}, use_global_device_ids=true | all-gather | bytes 1536 | tf_op jit(solution)/shard_map/all_gather | solution.py:15
  251.8 12.8 %all-gather.19 = f32[2,1,128]{2,1,0:T(1,128)S(1)} all-gather(f32[1,1,128]{2,1,0:T(1,128)S(1)} %bitcast.152), channel_id=6, replica_groups=mesh['row_0'=2,'row_1'=4,'col_0'=8,'col_1'=2,'col_2'=2] {'col_2'}, dimensions={0}, use_global_device_ids=true | all-gather | bytes 1536 | tf_op jit(solution)/shard_map/all_gather | solution.py:15
  265.1 10.4 %all-gather.22 = f32[8,1,128]{2,1,0:T(1,128)S(1)} all-gather(f32[1,1,128]{2,1,0:T(1,128)S(1)} %bitcast.146), channel_id=9, replica_groups=mesh['row_0'=2,'row_1'=4,'col_0'=8,'col_1'=2,'col_2'=2] {'col_0'}, dimensions={0}, use_global_device_ids=true | all-gather | bytes 4608 | tf_op jit(solution)/shard_map/all_gather | solution.py:15
  275.6 4.6 %all-gather.23 = f32[2,1,128]{2,1,0:T(1,128)S(1)} all-gather(f32[1,1,128]{2,1,0:T(1,128)S(1)} %bitcast.151), channel_id=10, replica_groups=mesh['row_0'=2,'row_1'=4,'col_0'=8,'col_1'=2,'col_2'=2] {'col_1'}, dimensions={0}, use_global_device_ids=true | all-gather | bytes 1536 | tf_op jit(solution)/shard_map/all_gather | solution.py:15
  280.2 6.7 %all-gather.24 = f32[2,1,128]{2,1,0:T(1,128)S(1)} all-gather(f32[1,1,128]{2,1,0:T(1,128)S(1)} %bitcast.153), channel_id=11, replica_groups=mesh['row_0'=2,'row_1'=4,'col_0'=8,'col_1'=2,'col_2'=2] {'col_2'}, dimensions={0}, use_global_device_ids=true | all-gather | bytes 1536 | tf_op jit(solution)/shard_map/all_gather | solution.py:15
  288.0 7.7 %all-to-all-start.7 = ((f32[32,4,128]{2,1,0:T(4,128)}), f32[32,4,128]{2,1,0:T(4,128)S(1)}, u32[]{:S(2)}, u32[]{:S(2)}) async-start(f32[32,4,128]{2,1,0:T(4,128)} %bitcast.50), calls=%async_computation.7 | async-start | bytes 131072 | tf_op jit(solution)/shard_map/all_to_all | solution.py:26
  297.1 8.5 %all-to-all-done.7 = f32[32,4,128]{2,1,0:T(4,128)S(1)} async-done(((f32[32,4,128]{2,1,0:T(4,128)}), f32[32,4,128]{2,1,0:T(4,128)S(1)}, u32[]{:S(2)}, u32[]{:S(2)}) %all-to-all-start.7) | async-done | bytes 65568 | tf_op jit(solution)/shard_map/all_to_all | solution.py:26
  (142 shorter events, 73.4 us)
Async XLA Ops:
  0.6 1.6 copy-start
  0.6 1.2 copy-start.1
  2.1 0.7 copy-start.3
  2.2 0.7 copy-start.6
  2.8 1.0 copy-start.7
  3.9 0.8 copy-start.2
  39.3 3.5 %copy-start.4 = (s32[32,8]{0,1:T(8,128)S(1)}, s32[32,8]{0,1:T(8,128)}, u32[]{:S(2)}) copy-start(s32[32,8]{0,1:T(8,128)} %param.14) | copy-start | bytes 3076
  39.3 8.6 %all-to-all-start.2 = ((f32[8,4,1,512]{3,1,2,0:T(4,128)}), f32[8,4,1,512]{3,1,2,0:T(4,128)S(1)}, u32[]{:S(2)}, u32[]{:S(2)}) async-start(f32[8,4,1,512]{3,1,2,0:T(4,128)} %copy.110), calls=%async_computation.2 | async-start | bytes 131072 | tf_op jit(solution)/shard_map/all_to_all | solution.py:76
  42.8 0.7 copy-start.5
  43.6 0.7 copy-start.12
  50.5 1.4 copy-start.11
  58.9 1.4 copy-start.10
  70.4 1.4 copy-start.9
  86.1 1.4 copy-start.8
  134.8 8.5 %all-to-all-start.5 = ((f32[8,4,1,512]{3,1,2,0:T(4,128)}), f32[8,4,1,512]{3,1,2,0:T(4,128)S(1)}, u32[]{:S(2)}, u32[]{:S(2)}) async-start(f32[8,4,1,512]{3,1,2,0:T(4,128)} %copy.116), calls=%async_computation.5 | async-start | bytes 131072 | tf_op jit(solution)/shard_map/all_to_all | solution.py:76
  151.2 16.6 %all-to-all-start.8 = ((f32[8,64,128]{2,1,0:T(8,128)}), f32[8,64,128]{2,1,0:T(8,128)S(1)}, u32[]{:S(2)}, u32[]{:S(2)}) async-start(f32[8,64,128]{2,1,0:T(8,128)} %fusion.7), calls=%async_computation.8 | async-start | bytes 524288 | tf_op jit(solution)/shard_map/all_to_all | solution.py:26
  167.8 23.7 %all-to-all-start.6 = ((f32[8,128,128]{2,1,0:T(8,128)}), f32[8,128,128]{2,1,0:T(8,128)S(1)}, u32[]{:S(2)}, u32[]{:S(2)}) async-start(f32[8,128,128]{2,1,0:T(8,128)} %fusion.9), calls=%async_computation.6 | async-start | bytes 1048576 | tf_op jit(solution)/shard_map/all_to_all | solution.py:26
  191.5 96.6 %all-to-all-start.9 = ((f32[32,2,128]{2,1,0:T(2,128)}), f32[32,2,128]{2,1,0:T(2,128)S(1)}, u32[]{:S(2)}, u32[]{:S(2)}) async-start(f32[32,2,128]{2,1,0:T(2,128)} %bitcast.54), calls=%async_computation.9 | async-start | bytes 65536 | tf_op jit(solution)/shard_map/all_to_all | solution.py:26
  288.0 17.6 %all-to-all-start.7 = ((f32[32,4,128]{2,1,0:T(4,128)}), f32[32,4,128]{2,1,0:T(4,128)S(1)}, u32[]{:S(2)}, u32[]{:S(2)}) async-start(f32[32,4,128]{2,1,0:T(4,128)} %bitcast.50), calls=%async_computation.7 | async-start | bytes 131072 | tf_op jit(solution)/shard_map/all_to_all | solution.py:26
